TPU v7x, 256 devices: a whole 4x4x8 slice. The times are simulated.
256 devices in a mesh: mem: 8 (over x, core), band: 32 (over y, z).
Axes of the slice: x: 4, y: 4, z: 8, core: 2. Of those that a mesh axis runs over, the one named last changes fastest.
Arguments:
- sample_collection: float32 [48, 3, 256, 4096], P('mem', None, 'band'), may hold values from -6 to 6
- seabed_profile: float32 [256, 4096], P('band'), may hold values from 0.5 to 2
- gauge_grid_position: int32 [128, 128], P('band'), may hold values from 0 to 1048575, as said below
- observed_values: float32 [128, 128], P('band'), may hold values from -6 to 6
- error_scale: float32 [128, 128], P('band'), may hold values from 0.3 to 3
- perturbation: float32 [48, 128, 128], P('mem', 'band'), may hold values from -6 to 6
- inflation: float32 [1], replicated, may hold values from 1 to 16
Outputs:
- analysis: float32 [48, 3, 256, 4096], P('mem', None, 'band')
Inputs may be any that keep to these rules, and one draw needn't show every extreme that they name: Every entry in row r of gauge_grid_position lies in grid rows b * 8 to (b + 1) * 8 - 1 with b = r // 4; cells may repeat.
All inputs are finite; a program needn't handle non-finite values.
Results may differ from a plain program's by a relative error of at most 0.000071.
Values sent between devices are 32-bit elements; how exact they have to be, the bound alone decides.
A program may use at most 128 MiB of HBM per device.

v0:
```python
import math

import jax
import jax.numpy as jnp
from jax import lax
from jax.sharding import PartitionSpec as P

STEPS = 2


courant = 0.5
coriolis_base = 0.15
coriolis_slope = 0.3


def with_halo(cells, sides, width):
    for axis, dim in sides:
        count = lax.axis_size(axis)
        ends = count - 1
        head = lax.slice_in_dim(cells, 0, width, axis=dim)
        tail = lax.slice_in_dim(cells, cells.shape[dim] - width, cells.shape[dim], axis=dim)
        cells = jnp.concatenate(
            [
                lax.ppermute(tail, axis, [(i, (i + 1) % count) for i in range(ends)]),
                cells,
                lax.ppermute(head, axis, [((i + 1) % count, i) for i in range(ends)]),
            ],
            axis=dim,
        )
    return cells


def side_by_side(arrays, axis, dim, along):
    widths = [a.shape[along] for a in arrays]
    both = jnp.concatenate(arrays, axis=along)
    whole = lax.all_gather(both, axis, axis=dim, tiled=True)
    return tuple(jnp.split(whole, [sum(widths[:k]) for k in range(1, len(widths))], axis=along))


def sent_to_all(x, axis):
    length = lax.axis_size(axis)
    return lax.all_to_all(jnp.broadcast_to(x[None], (length, *x.shape)), axis, 0, 0, tiled=True)


def taken_together(x, axis):
    return sent_to_all(x, axis).sum(axis=0)


def in_one(arrays, axis):
    ends = [0]
    for a in arrays:
        ends.append(ends[-1] + a.size)
    subtotal = taken_together(jnp.concatenate([a.ravel() for a in arrays]), axis)
    return tuple((subtotal[b:e].reshape(a.shape) for a, b, e in zip(arrays, ends, ends[1:])))


def east_diff(quantity):
    return (jnp.roll(quantity, -1, axis=-1) - jnp.roll(quantity, 1, axis=-1)) * 0.5


def body(
    sample_collection,
    seabed_profile,
    gauge_grid_position,
    observed_values,
    error_scale,
    perturbation,
    inflation,
):
    local_members, _, band_rows, columns = sample_collection.shape
    total_rows = band_rows * lax.axis_size("band")
    sample_trajectories = local_members * lax.axis_size("mem")
    first_row = lax.axis_index("band") * band_rows
    global_rows = (first_row + jnp.arange(band_rows)).astype(jnp.float32)
    earth_spin_turning = (coriolis_base + coriolis_slope * (global_rows + 0.5) / total_rows)[
        :, None
    ]
    surface_height, eastward_velocity_field, northward_velocity_field = (
        sample_collection[:, 0],
        sample_collection[:, 1],
        sample_collection[:, 2],
    )
    for _ in range(STEPS):
        rim_flux = with_halo(seabed_profile * northward_velocity_field, (("band", 1),), 1)
        surface_height = surface_height - courant * (
            east_diff(seabed_profile * eastward_velocity_field)
            + (rim_flux[:, 2:] - rim_flux[:, :-2]) * 0.5
        )
        eastward_velocity_field = (
            eastward_velocity_field
            - courant * east_diff(surface_height)
            + earth_spin_turning * northward_velocity_field
        )
        rim_height = with_halo(surface_height, (("band", 1),), 1)
        northward_velocity_field = (
            northward_velocity_field
            - courant * ((rim_height[:, 2:] - rim_height[:, :-2]) * 0.5)
            - earth_spin_turning * eastward_velocity_field
        )
    prior_model_outputs = jnp.stack(
        [surface_height, eastward_velocity_field, northward_velocity_field], axis=1
    )
    local_cells = gauge_grid_position.reshape(-1) - first_row * columns
    modelled_water_levels = jnp.take(surface_height.reshape(local_members, -1), local_cells, axis=1)
    obs_scale = error_scale.reshape(-1)
    factor = inflation[0]
    innovation = (
        observed_values.reshape(-1)
        + jnp.sqrt(factor) * obs_scale * perturbation.reshape(local_members, -1)
        - modelled_water_levels
    ) / obs_scale
    norm_factor = math.sqrt(sample_trajectories - 1)
    predicted_all, innovation_all = side_by_side((modelled_water_levels, innovation), "mem", 0, 1)
    centre = jnp.sum(predicted_all, axis=0) / sample_trajectories
    spread = (predicted_all - centre) / (obs_scale * norm_factor)
    gram_local = jnp.dot(
        spread, spread.T, precision=lax.Precision.HIGHEST, preferred_element_type=jnp.float32
    )
    cross_local = jnp.dot(
        spread,
        innovation_all.T,
        precision=lax.Precision.HIGHEST,
        preferred_element_type=jnp.float32,
    )
    gram_matrix, cross_term = in_one((gram_local, cross_local), "band")
    system = gram_matrix + factor * jnp.eye(sample_trajectories, dtype=jnp.float32)
    cholesky_lower = jnp.linalg.cholesky(system)
    middle = lax.linalg.triangular_solve(cholesky_lower, cross_term, left_side=True, lower=True)
    weights = lax.linalg.triangular_solve(
        cholesky_lower, middle, left_side=True, lower=True, transpose_a=True
    )
    assimilate_update_step = (
        jnp.eye(sample_trajectories, dtype=jnp.float32)
        + (weights - jnp.mean(weights, axis=0, keepdims=True)) / norm_factor
    )
    own_rows = lax.dynamic_slice_in_dim(
        assimilate_update_step, lax.axis_index("mem") * local_members, local_members, 0
    )
    return lax.psum_scatter(
        jnp.tensordot(
            own_rows, prior_model_outputs, axes=([0], [0]), precision=lax.Precision.HIGHEST
        ),
        "mem",
        scatter_dimension=0,
        tiled=True,
    )


def solution(mesh):
    in_specs = (
        P("mem", None, "band", None),
        P("band", None),
        P("band", None),
        P("band", None),
        P("band", None),
        P("mem", "band", None),
        P(),
    )
    out_specs = P("mem", None, "band", None)
    return jax.shard_map(body, mesh=mesh, in_specs=in_specs, out_specs=out_specs, check_vma=False)
```

profile of v0, /device:TPU:1, one launch (start us, length us, event | category | flops | bytes accessed | tf_op | source)
XLA Modules:
  0.0 274.5 jit_solution(8361007433853086543)
XLA Ops:
  6.5 2.7 fusion.58
  9.3 0.0 copy-done
  9.3 0.9 fusion.31
  10.2 0.0 copy-start.4
  10.2 0.0 copy-start.2
  10.3 1.3 collective-permute-start
  11.6 5.0 %collective-permute-start.1 = (f32[6,1,4096]{2,0,1:T(8,128)S(1)}, f32[6,1,4096]{2,0,1:T(8,128)S(1)}, u32[]{:S(2)}, u32[]{:S(2)}) collective-permute-start(f32[6,1,4096]{2,0,1:T(8,128)S(1)} %get-tuple-element.41), channel_id=1, source_target_pairs={{0,1},{1,2},{2,3},{3,4},{4,5},{5,6},{6,7},{7,8},{8,9},{9,10},{10,1... | collective-permute-start | bytes 294920 | tf_op jit(solution)/shard_map/ppermute | solution.py:24
  16.6 0.1 fusion.68
  16.7 1.7 fusion.69
  19.1 0.0 copy-done.4
  19.1 0.0 copy-done.2
  19.1 0.0 collective-permute-done
  19.2 0.0 collective-permute-done.1
  19.2 2.6 fusion.22
  21.8 0.1 fusion.67
  21.9 0.3 fusion.66
  22.2 1.3 collective-permute-start.2
  23.5 4.2 %collective-permute-start.3 = (f32[6,1,4096]{2,0,1:T(8,128)S(1)}, f32[6,1,4096]{2,0,1:T(8,128)S(1)}, u32[]{:S(2)}, u32[]{:S(2)}) collective-permute-start(f32[6,1,4096]{2,0,1:T(8,128)S(1)} %get-tuple-element.31), channel_id=1, source_target_pairs={{0,1},{1,2},{2,3},{3,4},{4,5},{5,6},{6,7},{7,8},{8,9},{9,10},{10,1... | collective-permute-start | bytes 294920 | tf_op jit(solution)/shard_map/ppermute | solution.py:24
  27.7 1.3 broadcast_multiply_fusion.1
  29.0 0.3 fusion.63
  29.3 0.0 collective-permute-done.2
  29.4 0.3 collective-permute-done.3
  29.7 1.7 broadcast_multiply_fusion
  31.4 1.3 collective-permute-start.4
  32.7 4.4 %collective-permute-start.5 = (f32[6,1,4096]{2,0,1:T(8,128)S(1)}, f32[6,1,4096]{2,0,1:T(8,128)S(1)}, u32[]{:S(2)}, u32[]{:S(2)}) collective-permute-start(f32[6,1,4096]{2,0,1:T(8,128)S(1)} %get-tuple-element.29), channel_id=1, source_target_pairs={{0,1},{1,2},{2,3},{3,4},{4,5},{5,6},{6,7},{7,8},{8,9},{9,10},{10,1... | collective-permute-start | bytes 294920 | tf_op jit(solution)/shard_map/ppermute | solution.py:24
  37.1 0.1 fusion.62
  37.2 0.3 collective-permute-done.4
  37.5 1.5 collective-permute-done.5
  39.1 0.5 fusion.14
  39.6 1.7 fusion.59
  41.3 9.0 %copy.56 = f32[6,32768]{0,1:T(8,128)} copy(f32[6,32768]{1,0:T(8,128)S(1)} %bitcast.76) | data formatting | bytes 1572864 | tf_op jit(solution)/shard_map/reshape | solution.py:104
  50.2 6.8 %gather_fusion = f32[512,6]{1,0:T(8,128)S(1)} fusion(f32[6,32768]{0,1:T(8,128)} %copy.56, s32[1024]{0:T(1024)S(1)} %pad_clamp_fusion), kind=kCustom, calls=%fused_computation | custom fusion | bytes 26624 | tf_op jit(solution)/shard_map/jit(_take)/gather | solution.py:104
  57.0 0.1 copy.57
  57.2 0.0 copy-done.1
  57.2 0.0 copy-done.3
  57.2 17.9 %all-gather = f32[8,6,1024]{2,1,0:T(8,128)S(1)} all-gather(f32[1,6,1024]{2,1,0:T(8,128)S(1)} %maximum_bitcast_fusion), channel_id=1, replica_groups=mesh['mem'=8,'band'=32] {'mem'}, dimensions={0}, use_global_device_ids=true | all-gather | bytes 221184 | tf_op jit(solution)/shard_map/all_gather | solution.py:36
  75.2 0.2 fusion.32
  75.4 0.2 fusion.34
  75.7 1.3 collective-permute-start.6
  77.0 4.7 %collective-permute-start.7 = (f32[6,1,4096]{2,0,1:T(8,128)S(1)}, f32[6,1,4096]{2,0,1:T(8,128)S(1)}, u32[]{:S(2)}, u32[]{:S(2)}) collective-permute-start(f32[6,1,4096]{2,0,1:T(8,128)S(1)} %get-tuple-element.23), channel_id=1, source_target_pairs={{0,1},{1,2},{2,3},{3,4},{4,5},{5,6},{6,7},{7,8},{8,9},{9,10},{10,1... | collective-permute-start | bytes 294920 | tf_op jit(solution)/shard_map/ppermute | solution.py:24
  81.7 0.1 reshape.115
  81.7 0.1 reshape.116
  81.8 1.1 broadcast_in_dim.15
  83.0 17.0 %all-to-all-start = ((f32[32,1,4608]{2,1,0:T(1,128)}), f32[32,1,4608]{2,1,0:T(1,128)}, u32[]{:S(2)}, u32[]{:S(2)}) async-start(f32[32,1,4608]{2,1,0:T(1,128)} %broadcast_in_dim.15), calls=%async_computation | async-start | bytes 1179648 | tf_op jit(solution)/shard_map/all_to_all | solution.py:42
  100.0 0.2 reduce-scatter.2.cloned.1.call-start
  100.2 0.1 fusion.60
  100.3 0.0 collective-permute-done.6
  100.3 0.0 collective-permute-done.7
  100.3 3.4 %fusion.10 = (f32[6,1,8,4096]{3,0,2,1:T(8,128)S(1)}, f32[6,8,4096]{2,0,1:T(8,128)}) fusion(f32[6,8,4096]{2,0,1:T(8,128)} %get-tuple-element.14, f32[6,8,4096]{2,0,1:T(8,128)S(1)} %fusion.14, f32[6,1,4096]{2,0,1:T(8,128)S(1)} %collective-permute-done.7, f32[6,1,4096]{2,0,1:T(8,128)S(1)} %collective-permute-done.6, f32[8]{0:T(128)S(1)} %multiply_add_fusion, ...), kind=kLoop, calls=%fused_computation.12 | loop fusion | flops 2752512 | bytes 5701664 | tf_op jit(solution)/shard_map/stack | solution.py:100
  103.7 11.5 %all-to-all-done = f32[32,1,4608]{2,1,0:T(1,128)} async-done(((f32[32,1,4608]{2,1,0:T(1,128)}), f32[32,1,4608]{2,1,0:T(1,128)}, u32[]{:S(2)}, u32[]{:S(2)}) %all-to-all-start) | async-done | bytes 589856 | tf_op jit(solution)/shard_map/all_to_all | solution.py:42
  115.3 1.4 reduce_sum.28
  116.7 0.1 reshape.117
  116.8 0.1 copy.59
  116.9 4.4 %cholesky.13 = f32[48,48]{1,0:T(8,128)S(1)} custom-call(f32[48,48]{1,0:T(8,128)S(1)} %fusion.40), custom_call_target="Cholesky" | custom-call | tf_op jit(solution)/shard_map/jit(cholesky)/cholesky | solution.py:127
  121.3 0.7 compare_reduce_fusion
  122.0 0.6 fusion.35
  122.6 3.7 %custom-call.8 = f32[1,48,48]{1,2,0:T(8,128)S(1)} custom-call(f32[1,48,48]{2,1,0:T(8,128)S(1)} %fusion.35), custom_call_target="InvertDiagBlocksLowerTriangular" | custom-call | tf_op jit(solution)/shard_map/triangular_solve | solution.py:129
  126.3 0.1 reshape.118
  126.4 0.2 fusion.38
  126.6 0.2 fusion.72
  126.8 16.2 %fusion = f32[48,3,8,4096]{3,0,2,1:T(8,128)S(1)} fusion(f32[6,1,8,4096]{3,0,2,1:T(8,128)S(1)} %get-tuple-element.9, f32[6,1,8,4096]{3,0,2,1:T(8,128)} %bitcast.78, f32[6,1,8,4096]{3,0,2,1:T(8,128)S(1)} %bitcast.77, f32[48,48]{1,0:T(8,128)S(1)} %get-tuple-element.49, s32[]{:T(128)S(6)} %select_n.31, pred[48,48]{1,0:T(8,128)(4,1)S(1)} %iota_compare_fusion.1, ...), kind=kOutput, calls=%fused_computation.1 | convolution fusion | flops 340919424 | bytes 21763588 | tf_op jit(solution)/shard_map/dot_general | solution.py:140
  143.0 21.1 %copy.60 = f32[48,3,8,4096]{3,2,1,0:T(8,128)} copy(f32[48,3,8,4096]{3,0,2,1:T(8,128)S(1)} %fusion) | data formatting | bytes 37748736 | tf_op jit(solution)/shard_map/dot_general | solution.py:140
  164.1 0.0 reduce-scatter.2.cloned.1.call-update
  164.1 103.5 %reduce-scatter.2.cloned.1.call-done = f32[6,3,8,4096]{3,2,1,0:T(8,128)} async-done(((f32[48,3,8,4096]{3,2,1,0:T(8,128)}), f32[6,3,8,4096]{3,2,1,0:T(8,128)}) %reduce-scatter.2.cloned.1.call-update) | async-done | bytes 2359312 | tf_op jit(solution)/shard_map/reduce_scatter | solution.py:139
  (24 shorter events, 0.3 us)
Async XLA Ops:
  6.5 2.7 copy-start
  10.2 8.8 %copy-start.4 = (s32[4,128]{1,0:T(4,128)S(1)}, s32[4,128]{1,0:T(4,128)}, u32[]{:S(2)}) copy-start(s32[4,128]{1,0:T(4,128)} %param.9) | copy-start | bytes 6148
  10.2 8.9 %copy-start.2 = (f32[4,128]{1,0:T(4,128)S(1)}, f32[4,128]{1,0:T(4,128)}, u32[]{:S(2)}) copy-start(f32[4,128]{1,0:T(4,128)} %param.11) | copy-start | bytes 6148
  10.3 8.9 %collective-permute-start = (f32[6,1,4096]{2,0,1:T(8,128)S(1)}, f32[6,1,4096]{2,0,1:T(8,128)S(1)}, u32[]{:S(2)}, u32[]{:S(2)}) collective-permute-start(f32[6,1,4096]{2,0,1:T(8,128)S(1)} %get-tuple-element.40), channel_id=1, source_target_pairs={{1,0},{2,1},{3,2},{4,3},{5,4},{6,5},{7,6},{8,7},{9,8},{10,9},{11,1... | collective-permute-start | bytes 294920 | tf_op jit(solution)/shard_map/ppermute | solution.py:26
  11.6 7.6 %collective-permute-start.1 = (f32[6,1,4096]{2,0,1:T(8,128)S(1)}, f32[6,1,4096]{2,0,1:T(8,128)S(1)}, u32[]{:S(2)}, u32[]{:S(2)}) collective-permute-start(f32[6,1,4096]{2,0,1:T(8,128)S(1)} %get-tuple-element.41), channel_id=1, source_target_pairs={{0,1},{1,2},{2,3},{3,4},{4,5},{5,6},{6,7},{7,8},{8,9},{9,10},{10,1... | collective-permute-start | bytes 294920 | tf_op jit(solution)/shard_map/ppermute | solution.py:24
  22.2 7.1 %collective-permute-start.2 = (f32[6,1,4096]{2,0,1:T(8,128)S(1)}, f32[6,1,4096]{2,0,1:T(8,128)S(1)}, u32[]{:S(2)}, u32[]{:S(2)}) collective-permute-start(f32[6,1,4096]{2,0,1:T(8,128)S(1)} %get-tuple-element.30), channel_id=1, source_target_pairs={{1,0},{2,1},{3,2},{4,3},{5,4},{6,5},{7,6},{8,7},{9,8},{10,9},{11,1... | collective-permute-start | bytes 294920 | tf_op jit(solution)/shard_map/ppermute | solution.py:26
  23.5 6.1 %collective-permute-start.3 = (f32[6,1,4096]{2,0,1:T(8,128)S(1)}, f32[6,1,4096]{2,0,1:T(8,128)S(1)}, u32[]{:S(2)}, u32[]{:S(2)}) collective-permute-start(f32[6,1,4096]{2,0,1:T(8,128)S(1)} %get-tuple-element.31), channel_id=1, source_target_pairs={{0,1},{1,2},{2,3},{3,4},{4,5},{5,6},{6,7},{7,8},{8,9},{9,10},{10,1... | collective-permute-start | bytes 294920 | tf_op jit(solution)/shard_map/ppermute | solution.py:24
  31.4 6.1 %collective-permute-start.4 = (f32[6,1,4096]{2,0,1:T(8,128)S(1)}, f32[6,1,4096]{2,0,1:T(8,128)S(1)}, u32[]{:S(2)}, u32[]{:S(2)}) collective-permute-start(f32[6,1,4096]{2,0,1:T(8,128)S(1)} %get-tuple-element.28), channel_id=1, source_target_pairs={{1,0},{2,1},{3,2},{4,3},{5,4},{6,5},{7,6},{8,7},{9,8},{10,9},{11,1... | collective-permute-start | bytes 294920 | tf_op jit(solution)/shard_map/ppermute | solution.py:26
  32.7 6.3 %collective-permute-start.5 = (f32[6,1,4096]{2,0,1:T(8,128)S(1)}, f32[6,1,4096]{2,0,1:T(8,128)S(1)}, u32[]{:S(2)}, u32[]{:S(2)}) collective-permute-start(f32[6,1,4096]{2,0,1:T(8,128)S(1)} %get-tuple-element.29), channel_id=1, source_target_pairs={{0,1},{1,2},{2,3},{3,4},{4,5},{5,6},{6,7},{7,8},{8,9},{9,10},{10,1... | collective-permute-start | bytes 294920 | tf_op jit(solution)/shard_map/ppermute | solution.py:24
  41.3 15.9 %copy-start.1 = (f32[6,4,128]{2,1,0:T(4,128)S(1)}, f32[6,4,128]{2,1,0:T(4,128)}, u32[]{:S(2)}) copy-start(f32[6,4,128]{2,1,0:T(4,128)} %param.12) | copy-start | bytes 36868
  41.3 15.9 %copy-start.3 = (f32[4,128]{1,0:T(4,128)S(1)}, f32[4,128]{1,0:T(4,128)}, u32[]{:S(2)}) copy-start(f32[4,128]{1,0:T(4,128)} %param.10) | copy-start | bytes 6148
  75.7 24.7 %collective-permute-start.6 = (f32[6,1,4096]{2,0,1:T(8,128)S(1)}, f32[6,1,4096]{2,0,1:T(8,128)S(1)}, u32[]{:S(2)}, u32[]{:S(2)}) collective-permute-start(f32[6,1,4096]{2,0,1:T(8,128)S(1)} %get-tuple-element.22), channel_id=1, source_target_pairs={{1,0},{2,1},{3,2},{4,3},{5,4},{6,5},{7,6},{8,7},{9,8},{10,9},{11,1... | collective-permute-start | bytes 294920 | tf_op jit(solution)/shard_map/ppermute | solution.py:26
  77.0 23.4 %collective-permute-start.7 = (f32[6,1,4096]{2,0,1:T(8,128)S(1)}, f32[6,1,4096]{2,0,1:T(8,128)S(1)}, u32[]{:S(2)}, u32[]{:S(2)}) collective-permute-start(f32[6,1,4096]{2,0,1:T(8,128)S(1)} %get-tuple-element.23), channel_id=1, source_target_pairs={{0,1},{1,2},{2,3},{3,4},{4,5},{5,6},{6,7},{7,8},{8,9},{9,10},{10,1... | collective-permute-start | bytes 294920 | tf_op jit(solution)/shard_map/ppermute | solution.py:24
  83.0 32.3 %all-to-all-start = ((f32[32,1,4608]{2,1,0:T(1,128)}), f32[32,1,4608]{2,1,0:T(1,128)}, u32[]{:S(2)}, u32[]{:S(2)}) async-start(f32[32,1,4608]{2,1,0:T(1,128)} %broadcast_in_dim.15), calls=%async_computation | async-start | bytes 1179648 | tf_op jit(solution)/shard_map/all_to_all | solution.py:42
  100.0 167.6 %reduce-scatter.2.cloned.1.call-start = ((), (), s32[]{:S(2)}) async-start(), calls=%async_computation.2 | async-start | bytes 21233664 | tf_op jit(solution)/shard_map/reduce_scatter | solution.py:139
Sparse Core Ops, SparseCore 0:
  164.2 103.3 reduce-scatter.1
where the time goes:
time: 275 us; the launch traced here: 274 us
  waiting for transfers between devices  117 us (43%)
  local copies, waits for them, and re-layouts  45.7 us (17%)
  starting transfers between devices  40.7 us (15%)
  other arithmetic  21.4 us (8%)
  blocking collectives  17.9 us (7%)
  matrix products  17.1 us (6%)
  between operations  14.4 us (5%)
    reduce_scatter x1, waiting for transfers between devices, body(): lax.psum_scatter(jnp.tensordot(own_rows, prior_model_outputs, axes=([0],...  104 us
    dot_general x1, local copies, waits for them, and re-layouts, body(): jnp.tensordot(own_rows, prior_model_outputs, axes=([0], [0]), precision=l...  21.1 us
    ppermute x4, starting transfers between devices, with_halo(): lax.ppermute(tail, axis, [(i, (i + 1) % count) for i in range(ends)])  18.3 us
    all_gather x1, blocking collectives, side_by_side(): whole = lax.all_gather(both, axis, axis=dim, tiled=True)  17.9 us
    all_to_all x1, starting transfers between devices, sent_to_all(): lax.all_to_all(jnp.broadcast_to(x[None], (length, *x.shape)), axis, 0, 0,...  17 us
    dot_general x1, matrix products, body(): jnp.tensordot(own_rows, prior_model_outputs, axes=([0], [0]), precision=l...  16.2 us
    all_to_all x1, waiting for transfers between devices, sent_to_all(): lax.all_to_all(jnp.broadcast_to(x[None], (length, *x.shape)), axis, 0, 0,...  11.5 us
    reshape x1, local copies, waits for them, and re-layouts, body(): surface_height.reshape(local_members, -1)  8.98 us
  transfers between devices with their start and end apart: 10, of which 5 were waited for; matrix products, arithmetic and copies ran while one was open for 3% of the time, Pallas kernels for 0%

commit v1 on v0

v1 whole, which is shorter than its diff:
```python
import functools
import math

import jax
import jax.numpy as jnp
from jax import lax
from jax.experimental import pallas as pl
from jax.experimental.pallas import tpu as pltpu
from jax.sharding import PartitionSpec as P

MESH = pl.DeviceIdType.MESH
HIGHEST = lax.Precision.HIGHEST

coriolis_base = 0.15
coriolis_slope = 0.3
PAD = 8


def rows_of(shape):
    return lax.broadcasted_iota(jnp.int32, shape, 0)


def lanes_of(shape):
    return lax.broadcasted_iota(jnp.int32, shape, 1)


def east(q):
    n = q.shape[1]
    return pltpu.roll(q, n - 1, 1) - pltpu.roll(q, 1, 1)


def north(q, above, below):
    n = q.shape[0]
    row = rows_of(q.shape)
    after = jnp.where(row == n - 1, below, pltpu.roll(q, n - 1, 0))
    before = jnp.where(row == 0, above, pltpu.roll(q, 1, 0))
    return after - before


def nt(a, b, precision=None):
    return lax.dot_general(
        a, b, (((1,), (1,)), ((), ())), precision=precision, preferred_element_type=jnp.float32
    )


def kernel(
    nm, nb, gz,
    ens, depth, pos, obs, scale, pert, infl,
    out,
    st, dv, hs, hr, onehot, hb, pi, zb, yb, xb, mb, spread_rows,
    load_sem, hs_sem, hr_sem, as_sem, ar_sem, zs_sem, zr_sem, ys_sem, yr_sem,
    fs_sem, fr_sem, bs_sem, br_sem,
):
    _, members, rows, cols = st.shape
    n_obs = onehot.shape[1]
    width = cols // nm
    np_ = nm * PAD
    total = nm * members
    cells = total * rows
    gy = nb // gz
    norm = math.sqrt(total - 1)
    me, b = lax.axis_index("mem"), lax.axis_index("band")
    z, y = lax.rem(b, gz), lax.div(b, gz)

    @pl.loop(0, members)
    def _(m):
        pltpu.make_async_copy(ens.at[m], st.at[:, m], load_sem.at[m]).start()

    barrier = pltpu.get_barrier_semaphore()
    for s in range(1, nm):
        pl.semaphore_signal(barrier, 1, device_id={"mem": lax.rem(me + s, nm)}, device_id_type=MESH)
    for s in range(1, gz):
        peer = y * gz + lax.rem(z + s, gz)
        pl.semaphore_signal(barrier, 1, device_id={"band": peer}, device_id_type=MESH)
    for s in range(1, gy):
        peer = lax.rem(y + s, gy) * gz + z
        pl.semaphore_signal(barrier, 1, device_id={"band": peer}, device_id_type=MESH)
    far_above = jnp.logical_and(z == 0, y > 0)
    far_below = jnp.logical_and(z == gz - 1, y < gy - 1)

    @pl.when(far_above)
    def _():
        pl.semaphore_signal(barrier, 1, device_id={"band": b - 1}, device_id_type=MESH)

    @pl.when(far_below)
    def _():
        pl.semaphore_signal(barrier, 1, device_id={"band": b + 1}, device_id_type=MESH)

    @pl.when(b == 0)
    def _():
        hr[:, 0] = jnp.zeros_like(hr[:, 0])

    @pl.when(b == nb - 1)
    def _():
        hr[:, 1] = jnp.zeros_like(hr[:, 1])

    def flat(x):
        return jnp.concatenate([x[q : q + 1, :] for q in range(x.shape[0])], axis=1)

    local = flat(pos[...]) - b * (rows * cols)
    obs_row = lax.shift_right_logical(local, int(math.log2(cols)))
    obs_col = jnp.bitwise_and(local, cols - 1)
    step = 256

    @pl.loop(0, cols // step)
    def _(k):
        col = rows_of((step, n_obs)) + k * step
        onehot[pl.ds(pl.multiple_of(k * step, step), step), :] = jnp.where(
            col == obs_col, 1.0, 0.0
        ).astype(jnp.bfloat16)

    j = lax.shift_right_logical(rows_of((cells, np_)), int(math.log2(rows)))
    padded = j
    for k in range(1, nm):
        padded = padded + jnp.where(j >= k * members, PAD - members, 0)
    spread_rows[...] = jnp.where(lanes_of((cells, np_)) == padded, 1.0, 0.0).astype(jnp.bfloat16)

    turn = coriolis_base + coriolis_slope * (
        (rows_of((rows, cols)) + b * rows).astype(jnp.float32) + 0.5
    ) / (nb * rows)
    inner_above = jnp.where(b > 0, 0.25, 0.0)
    inner_below = jnp.where(b < nb - 1, 0.25, 0.0)

    pl.semaphore_wait(
        barrier,
        nm - 1 + gz - 1 + gy - 1 + jnp.where(far_above, 1, 0) + jnp.where(far_below, 1, 0),
    )

    def halo(t, side, m):
        return pltpu.make_async_remote_copy(
            src_ref=hs.at[t, side, m],
            dst_ref=hr.at[t, 1 - side, m],
            send_sem=hs_sem.at[t, side, m],
            recv_sem=hr_sem.at[t, 1 - side, m],
            device_id={"band": jnp.where(b > 0, b - 1, 0) if side == 0 else jnp.where(b < nb - 1, b + 1, b)},
            device_id_type=MESH,
        )

    def begin(t, m, h, u, v):
        d = depth[...]
        flux = d * v
        part = h - 0.25 * east(d * u)
        dv[m] = flux
        st[0, m] = part
        hs[t, 0, m, 0:1, :] = flux[0:1]
        hs[t, 0, m, 1:2, :] = part[0:1] - 0.25 * flux[1:2]
        hs[t, 1, m, 0:1, :] = flux[rows - 1 : rows]
        hs[t, 1, m, 1:2, :] = part[rows - 1 : rows] + 0.25 * flux[rows - 2 : rows - 1]

        @pl.when(b > 0)
        def _():
            halo(t, 0, m).start()

        @pl.when(b < nb - 1)
        def _():
            halo(t, 1, m).start()

    def arrive(t, m):
        @pl.when(b > 0)
        def _():
            halo(t, 1, m).wait_recv()

        @pl.when(b < nb - 1)
        def _():
            halo(t, 0, m).wait_recv()

    def new_height(t, m):
        return st[0, m] - 0.25 * north(dv[m], hr[t, 0, m, 0:1, :], hr[t, 1, m, 0:1, :])

    def new_flow(t, m, h):
        flux = dv[m]
        above = hr[t, 0, m, 1:2, :] - inner_above * flux[0:1]
        below = hr[t, 1, m, 1:2, :] + inner_below * flux[rows - 1 : rows]
        v = st[2, m]
        u = st[1, m] - 0.25 * east(h) + turn * v
        v = v - 0.25 * north(h, above, below) - turn * u
        return u, v

    @pl.loop(0, members)
    def _(m):
        pltpu.make_async_copy(ens.at[m], st.at[:, m], load_sem.at[m]).wait()
        begin(0, m, st[0, m], st[1, m], st[2, m])

    @pl.loop(0, members)
    def _(m):
        arrive(0, m)
        h = new_height(0, m)
        u, v = new_flow(0, m, h)
        st[1, m] = u
        st[2, m] = v
        begin(1, m, h, u, v)

    @pl.loop(0, members)
    def _(m):
        arrive(1, m)
        st[0, m] = new_height(1, m)

    tall = members * rows
    kstep = 512

    def pick(k, acc):
        at = pl.ds(pl.multiple_of(k * kstep, kstep), kstep)
        h = st[0, :, :, at].reshape(tall, kstep)
        hi = h.astype(jnp.bfloat16)
        rest = h - hi.astype(jnp.float32)
        mid = rest.astype(jnp.bfloat16)
        low = (rest - mid.astype(jnp.float32)).astype(jnp.bfloat16)
        hb[0:tall] = hi
        hb[tall : 2 * tall] = mid
        hb[2 * tall : 3 * tall] = low
        return acc + jnp.dot(hb[...], onehot[at, :], preferred_element_type=jnp.float32)

    picked = lax.fori_loop(0, cols // kstep, pick, jnp.zeros((3 * tall, n_obs), jnp.float32))
    picked = picked[0:tall] + (picked[tall : 2 * tall] + picked[2 * tall : 3 * tall])
    here = rows_of((rows, n_obs)) == obs_row
    slot = rows_of((PAD, n_obs))
    predicted = jnp.zeros((PAD, n_obs), jnp.float32)
    noise = jnp.zeros((PAD, n_obs), jnp.float32)
    for m in range(members):
        mine = jnp.where(here, picked[m * rows : (m + 1) * rows], 0.0)
        predicted = jnp.where(slot == m, jnp.sum(mine, axis=0, keepdims=True), predicted)
        noise = jnp.where(slot == m, flat(pert[m]), noise)
    err = flat(scale[...])
    factor = jnp.full((1, n_obs), infl[0], jnp.float32)
    innovation = (flat(obs[...]) + jnp.sqrt(factor) * err * noise - predicted) / err
    pi[me, 0] = predicted
    pi[me, 1] = jnp.where(slot < members, innovation, 0.0)

    def gather(peer, src):
        return pltpu.make_async_remote_copy(
            src_ref=pi.at[src], dst_ref=pi.at[src], send_sem=as_sem.at[peer],
            recv_sem=ar_sem.at[src], device_id={"mem": peer}, device_id_type=MESH,
        )

    for s in range(1, nm):
        gather(lax.rem(me + s, nm), me).start()

    @pl.loop(0, members)
    def _(m):
        u, v = new_flow(1, m, st[0, m])
        st[1, m] = u
        st[2, m] = v

    own = pl.ds(pl.multiple_of(me * width, width), width)

    def forth(f, peer, src):
        at = pl.ds(pl.multiple_of(peer * width, width), width)
        return pltpu.make_async_remote_copy(
            src_ref=st.at[f, :, :, at], dst_ref=xb.at[f, src], send_sem=fs_sem.at[f, peer],
            recv_sem=fr_sem.at[f, src], device_id={"mem": peer}, device_id_type=MESH,
        )

    for f in range(3):
        for s in range(1, nm):
            forth(f, lax.rem(me + s, nm), me).start()
    for f in range(3):
        xb[f, me] = st[f, :, :, own]

    for s in range(1, nm):
        src = lax.rem(me + s, nm)
        gather(src, src).wait_recv()
    predicted = pi[:, 0].reshape(np_, n_obs)
    centre = jnp.sum(predicted, axis=0, keepdims=True) * (1.0 / total)
    inside = jnp.bitwise_and(rows_of((np_, n_obs)), PAD - 1) < members
    spread = jnp.where(inside, (predicted - centre) / (err * norm), 0.0)
    both = jnp.concatenate([spread, pi[:, 1].reshape(np_, n_obs)], axis=0)
    zb[z] = nt(spread, both, HIGHEST)

    def share(buf, send, recv, slot_, peer_slot, peer):
        return pltpu.make_async_remote_copy(
            src_ref=buf.at[slot_], dst_ref=buf.at[slot_], send_sem=send.at[peer_slot],
            recv_sem=recv.at[slot_], device_id={"band": peer}, device_id_type=MESH,
        )

    for s in range(1, gz):
        other = lax.rem(z + s, gz)
        share(zb, zs_sem, zr_sem, z, other, y * gz + other).start()
    for s in range(1, gz):
        other = lax.rem(z + s, gz)
        share(zb, zs_sem, zr_sem, other, other, y * gz + other).wait_recv()
    yb[y] = jnp.sum(zb[...], axis=0)
    for s in range(1, gy):
        other = lax.rem(y + s, gy)
        share(yb, ys_sem, yr_sem, y, other, other * gz + z).start()
    for s in range(1, gy):
        other = lax.rem(y + s, gy)
        share(yb, ys_sem, yr_sem, other, other, other * gz + z).wait_recv()
    system = jnp.sum(yb[...], axis=0)
    shape = (np_, 2 * np_)
    system = system + jnp.where(rows_of(shape) == lanes_of(shape), infl[0], 0.0)

    blocks = [system[k * PAD : (k + 1) * PAD] for k in range(nm)]
    sub = rows_of((PAD, 2 * np_))
    for k in range(total):
        home, r = divmod(k, members)
        p = home * PAD + r
        line = blocks[home][r : r + 1]
        line = line / line[:, p : p + 1]
        new = [x - x[:, p : p + 1] * line for x in blocks]
        new[home] = jnp.where(sub == r, line, new[home])
        blocks = new
    weights = jnp.concatenate([x[:, np_:] for x in blocks], axis=0)
    square = (np_, np_)
    mean = jnp.sum(weights, axis=0, keepdims=True) * (1.0 / total)
    transform = jnp.where(rows_of(square) == lanes_of(square), 1.0, 0.0) + (weights - mean) * (1.0 / norm)

    alike = jnp.bitwise_and(rows_of((cells, cells)), rows - 1) == jnp.bitwise_and(
        lanes_of((cells, cells)), rows - 1
    )

    def widen(t):
        grown = nt(spread_rows[...], t).astype(jnp.bfloat16)
        return jnp.where(alike, nt(grown, spread_rows[...]), 0.0).astype(jnp.bfloat16)

    hi = transform.astype(jnp.bfloat16)
    mix_hi = widen(hi)
    mix_lo = widen((transform - hi.astype(jnp.float32)).astype(jnp.bfloat16))

    def back(f, peer, src):
        at = pl.ds(pl.multiple_of(src * width, width), width)
        return pltpu.make_async_remote_copy(
            src_ref=mb.at[f, peer], dst_ref=out.at[:, f, :, at], send_sem=bs_sem.at[f, peer],
            recv_sem=br_sem.at[f, src], device_id={"mem": peer}, device_id_type=MESH,
        )

    for f in range(3):
        for s in range(1, nm):
            src = lax.rem(me + s, nm)
            forth(f, src, src).wait_recv()
        x = xb[f].reshape(cells, width)
        x_hi = x.astype(jnp.bfloat16)
        x_lo = (x - x_hi.astype(jnp.float32)).astype(jnp.bfloat16)
        mixed = jnp.dot(mix_hi, x_hi, preferred_element_type=jnp.float32) + (
            jnp.dot(mix_hi, x_lo, preferred_element_type=jnp.float32)
            + jnp.dot(mix_lo, x_hi, preferred_element_type=jnp.float32)
        )
        mb[f] = mixed.reshape(nm, members, rows, width)
        for s in range(1, nm):
            back(f, lax.rem(me + s, nm), me).start()
        out[:, f, :, own] = mb[f, me]

    @pl.loop(0, members)
    def _(m):
        for t in range(2):

            @pl.when(b > 0)
            def _():
                halo(t, 0, m).wait_send()

            @pl.when(b < nb - 1)
            def _():
                halo(t, 1, m).wait_send()

    for s in range(1, nm):
        gather(lax.rem(me + s, nm), me).wait_send()
    for s in range(1, gz):
        other = lax.rem(z + s, gz)
        share(zb, zs_sem, zr_sem, z, other, y * gz + other).wait_send()
    for s in range(1, gy):
        other = lax.rem(y + s, gy)
        share(yb, ys_sem, yr_sem, y, other, other * gz + z).wait_send()
    for f in range(3):
        for s in range(1, nm):
            peer = lax.rem(me + s, nm)
            forth(f, peer, me).wait_send()
    for f in range(3):
        for s in range(1, nm):
            peer = lax.rem(me + s, nm)
            back(f, peer, me).wait_send()
            back(f, peer, peer).wait_recv()


def body(ens, depth, pos, obs, scale, pert, infl):
    nm, nb = lax.axis_size("mem"), lax.axis_size("band")
    gz = 8 if nb >= 16 else 2
    gy = nb // gz
    members, fields, rows, cols = ens.shape
    n_obs = pos.size
    np_ = nm * PAD
    cells = nm * members * rows
    f32, bf16 = jnp.float32, jnp.bfloat16
    dma = pltpu.SemaphoreType.DMA
    vmem = pl.BlockSpec(memory_space=pltpu.VMEM)
    return pl.pallas_call(
        functools.partial(kernel, nm, nb, gz),
        out_shape=jax.ShapeDtypeStruct(ens.shape, f32),
        in_specs=[pl.BlockSpec(memory_space=pl.ANY)] + [vmem] * 5 + [pl.BlockSpec(memory_space=pltpu.SMEM)],
        out_specs=vmem,
        scratch_shapes=[
            pltpu.VMEM((fields, members, rows, cols), f32),
            pltpu.VMEM((members, rows, cols), f32),
            pltpu.VMEM((2, 2, members, 2, cols), f32),
            pltpu.VMEM((2, 2, members, 2, cols), f32),
            pltpu.VMEM((cols, n_obs), bf16),
            pltpu.VMEM((3 * members * rows, 512), bf16),
            pltpu.VMEM((nm, 2, PAD, n_obs), f32),
            pltpu.VMEM((gz, np_, 2 * np_), f32),
            pltpu.VMEM((gy, np_, 2 * np_), f32),
            pltpu.VMEM((fields, nm, members, rows, cols // nm), f32),
            pltpu.VMEM((fields, nm, members, rows, cols // nm), f32),
            pltpu.VMEM((cells, np_), bf16),
            dma((members,)),
            dma((2, 2, members)),
            dma((2, 2, members)),
            dma((nm,)),
            dma((nm,)),
            dma((gz,)),
            dma((gz,)),
            dma((gy,)),
            dma((gy,)),
            dma((fields, nm)),
            dma((fields, nm)),
            dma((fields, nm)),
            dma((fields, nm)),
        ],
        compiler_params=pltpu.CompilerParams(
            collective_id=0, has_side_effects=True, vmem_limit_bytes=48 * 1024 * 1024
        ),
        name="smoother",
    )(ens, depth, pos, obs, scale, pert, infl)


def solution(mesh):
    in_specs = (
        P("mem", None, "band", None),
        P("band", None),
        P("band", None),
        P("band", None),
        P("band", None),
        P("mem", "band", None),
        P(),
    )
    out_specs = P("mem", None, "band", None)
    return jax.shard_map(body, mesh=mesh, in_specs=in_specs, out_specs=out_specs, check_vma=False)
```

time: 275 us -> 87.5 us (0.32)
  waiting for transfers between devices: 117 us -> 0 us
  Pallas kernels: 0 us -> 79.9 us
  starting transfers between devices: 40.7 us -> 0 us
  local copies, waits for them, and re-layouts: 45.7 us -> 6.72 us
  other arithmetic: 21.4 us -> 0 us
  blocking collectives: 17.9 us -> 0 us
  matrix products: 17.1 us -> 0 us
  between operations: 14.4 us -> 0.67 us
    reduce_scatter x1 -> x0, waiting for transfers between devices: 104 us -> none  [body(): lax.psum_scatter(jnp.tensordot(own_rows, prior_model_outputs, axes=([0],...]
    pallas_call x0 -> x1, Pallas kernels: none -> 79.9 us  [body(): pl.pallas_call(functools.partial(kernel, nm, nb, gz), out_shape=jax.Shape...]
    ppermute x8 -> x0, starting transfers between devices: 23.5 us -> none  [the longest x4 18.3 us: with_halo(): lax.ppermute(tail, axis, [(i, (i + 1) % count) for i in range(ends)])]
    dot_general x1 -> x0, local copies, waits for them, and re-layouts: 21.1 us -> none  [body(): jnp.tensordot(own_rows, prior_model_outputs, axes=([0], [0]), precision=l...]
    all_gather x1 -> x0, blocking collectives: 17.9 us -> none  [side_by_side(): whole = lax.all_gather(both, axis, axis=dim, tiled=True)]
    all_to_all x1 -> x0, starting transfers between devices: 17 us -> none  [sent_to_all(): lax.all_to_all(jnp.broadcast_to(x[None], (length, *x.shape)), axis, 0, 0,...]
    dot_general x3 -> x0, matrix products: 16.7 us -> none  [the longest x1 16.2 us: body(): jnp.tensordot(own_rows, prior_model_outputs, axes=([0], [0]), precision=l...]
    another operation x6 -> x0, other arithmetic: 12.8 us -> none  [the longest x3 5.08 us: body(): cholesky_lower = jnp.linalg.cholesky(system)]
  transfers between devices with their start and end apart: 10 -> 0, of which waited for: 5 -> 0; matrix products, arithmetic and copies ran while one was open for 3% -> 0% of each run, Pallas kernels for 0% -> 0%
where the time goes in v1:
time: 87.5 us; the launch traced here: 87.3 us
  Pallas kernels  79.9 us (91%)
  local copies, waits for them, and re-layouts  6.72 us (8%)
    pallas_call x1, Pallas kernels, body(): pl.pallas_call(functools.partial(kernel, nm, nb, gz), out_shape=jax.Shape...  79.9 us
    unnamed x13, local copies, waits for them, and re-layouts  6.72 us

profile of v1, /device:TPU:1, one launch (start us, length us, event | category | flops | bytes accessed | tf_op | source)
XLA Modules:
  0.0 87.3 jit_solution(17394936376418961912)
XLA Ops:
  0.7 0.0 copy-start
  0.7 1.7 %copy-done = f32[6,3,8,4096]{3,2,1,0:T(8,128)S(1)} copy-done((f32[6,3,8,4096]{3,2,1,0:T(8,128)S(1)}, f32[6,3,8,4096]{3,2,1,0:T(8,128)}, u32[]{:S(2)}) %copy-start) | copy-done | bytes 2359320
  2.3 0.0 copy-start.1
  2.3 0.9 %copy-done.1 = f32[8,4096]{1,0:T(8,128)S(1)} copy-done((f32[8,4096]{1,0:T(8,128)S(1)}, f32[8,4096]{1,0:T(8,128)}, u32[]{:S(2)}) %copy-start.1) | copy-done | bytes 131096
  3.2 0.0 copy-start.2
  3.2 0.7 copy-done.2
  3.9 0.0 copy-start.3
  3.9 0.7 copy-done.3
  4.6 0.0 copy-start.4
  4.6 0.7 copy-done.4
  5.3 0.0 copy-start.5
  5.3 0.7 copy-done.5
  6.0 79.9 %smoother.1 = f32[6,3,8,4096]{3,2,1,0:T(8,128)S(1)} custom-call(f32[6,3,8,4096]{3,2,1,0:T(8,128)S(1)} %copy-done, f32[8,4096]{1,0:T(8,128)S(1)} %copy-done.1, s32[4,128]{1,0:T(4,128)S(1)} %copy-done.3, f32[4,128]{1,0:T(4,128)S(1)} %copy-done.4, f32[4,128]{1,0:T(4,128)S(1)} %copy-done.5, f32[6,4,128]{2,1,0:T(4,128)S(1)} %copy-done.2, f32[1]{0:T(128)S(6)} %copy.9.infl), custom_call_target="tpu_custom_call" | custom-call | tf_op jit(solution)/shard_map/smoother/pallas_call | solution.py:384
  85.9 1.4 %copy.10 = f32[6,3,8,4096]{3,2,1,0:T(8,128)} copy(f32[6,3,8,4096]{3,2,1,0:T(8,128)S(1)} %smoother.1) | data formatting | bytes 4718592
Async XLA Ops:
  0.7 1.7 %copy-start = (f32[6,3,8,4096]{3,2,1,0:T(8,128)S(1)}, f32[6,3,8,4096]{3,2,1,0:T(8,128)}, u32[]{:S(2)}) copy-start(f32[6,3,8,4096]{3,2,1,0:T(8,128)} %ens.1) | copy-start | bytes 7077892
  2.3 0.9 %copy-start.1 = (f32[8,4096]{1,0:T(8,128)S(1)}, f32[8,4096]{1,0:T(8,128)}, u32[]{:S(2)}) copy-start(f32[8,4096]{1,0:T(8,128)} %depth.1) | copy-start | bytes 393220
  3.2 0.7 copy-start.2
  3.9 0.7 copy-start.3
  4.6 0.7 copy-start.4
  5.3 0.7 copy-start.5

commit v2 on v1

v2 whole, which is shorter than its diff:
```python
import functools
import math

import jax
import jax.numpy as jnp
from jax import lax
from jax.experimental import pallas as pl
from jax.experimental.pallas import tpu as pltpu
from jax.sharding import PartitionSpec as P

MESH = pl.DeviceIdType.MESH
HIGHEST = lax.Precision.HIGHEST

coriolis_base = 0.15
coriolis_slope = 0.3
PAD = 8


def rows_of(shape):
    return lax.broadcasted_iota(jnp.int32, shape, 0)


def lanes_of(shape):
    return lax.broadcasted_iota(jnp.int32, shape, 1)


def east(q):
    n = q.shape[1]
    return pltpu.roll(q, n - 1, 1) - pltpu.roll(q, 1, 1)


def north(q, above, below):
    n = q.shape[0]
    row = rows_of(q.shape)
    after = jnp.where(row == n - 1, below, pltpu.roll(q, n - 1, 0))
    before = jnp.where(row == 0, above, pltpu.roll(q, 1, 0))
    return after - before


def nt(a, b, precision=None):
    return lax.dot_general(
        a, b, (((1,), (1,)), ((), ())), precision=precision, preferred_element_type=jnp.float32
    )


def kernel(
    nm, nb, gz,
    ens, depth_in, pos_in, obs_in, scale_in, pert_in, infl,
    out,
    depth, pos, obs, scale, pert,
    st, dv, hs, hr, onehot, hb, noise, pi, zb, yb, sb, xb, mb, spread_rows,
    load_sem, small_sem, hs_sem, hr_sem, ns_sem, nr_sem, as_sem, ar_sem, zs_sem, zr_sem, ys_sem, yr_sem,
    ss_sem, sr_sem, fs_sem, fr_sem, bs_sem, br_sem,
):
    _, members, rows, cols = st.shape
    n_obs = onehot.shape[1]
    width = cols // nm
    np_ = nm * PAD
    total = nm * members
    cells = total * rows
    gy = nb // gz
    norm = math.sqrt(total - 1)
    H, U, V = 0, 1, 2
    me, b = lax.axis_index("mem"), lax.axis_index("band")
    z, y = lax.rem(b, gz), lax.div(b, gz)
    mates = [lax.rem(me + s, nm) for s in range(1, nm)]

    small = [
        pltpu.make_async_copy(source, target, small_sem.at[k])
        for k, (source, target) in enumerate(
            [(depth_in, depth), (pos_in, pos), (obs_in, obs), (scale_in, scale), (pert_in, pert)]
        )
    ]
    load = [pltpu.make_async_copy(ens.at[:, f], st.at[f], load_sem.at[f]) for f in range(3)]
    small[0].start()
    load[V].start()
    small[4].start()
    load[U].start()
    load[H].start()
    for copy in small[1:4]:
        copy.start()

    barrier = pltpu.get_barrier_semaphore()

    def greet(where):
        pl.semaphore_signal(barrier, 1, device_id=where, device_id_type=MESH)

    for peer in mates:
        greet({"mem": peer})
    for s in range(1, gz):
        greet({"band": y * gz + lax.rem(z + s, gz)})
    for s in range(1, gy):
        greet({"band": lax.rem(y + s, gy) * gz + z})
    far_above = jnp.logical_and(z == 0, y > 0)
    far_below = jnp.logical_and(z == gz - 1, y < gy - 1)

    @pl.when(far_above)
    def _():
        greet({"band": b - 1})

    @pl.when(far_below)
    def _():
        greet({"band": b + 1})

    @pl.when(b == 0)
    def _():
        hr[:, 0] = jnp.zeros_like(hr[:, 0])

    @pl.when(b == nb - 1)
    def _():
        hr[:, 1] = jnp.zeros_like(hr[:, 1])

    def turn(lanes):
        row = (rows_of((rows, lanes)) + b * rows).astype(jnp.float32)
        return coriolis_base + coriolis_slope * (row + 0.5) / (nb * rows)

    def halo(t, side, m):
        return pltpu.make_async_remote_copy(
            src_ref=hs.at[t, side, m],
            dst_ref=hr.at[t, 1 - side, m],
            send_sem=hs_sem.at[t, side, m],
            recv_sem=hr_sem.at[t, 1 - side, m],
            device_id={"band": jnp.where(b > 0, b - 1, 0) if side == 0 else jnp.where(b < nb - 1, b + 1, b)},
            device_id_type=MESH,
        )

    def edges(t, m, q):
        hs[t, 0, m] = q[0:1]
        hs[t, 1, m] = q[rows - 1 : rows]

        @pl.when(b > 0)
        def _():
            halo(t, 0, m).start()

        @pl.when(b < nb - 1)
        def _():
            halo(t, 1, m).start()

    def arrive(t, m):
        @pl.when(b > 0)
        def _():
            halo(t, 1, m).wait_recv()

        @pl.when(b < nb - 1)
        def _():
            halo(t, 0, m).wait_recv()

    def tell(buf, send, recv, peer, src):
        return pltpu.make_async_remote_copy(
            src_ref=buf.at[src], dst_ref=buf.at[src], send_sem=send.at[peer],
            recv_sem=recv.at[src], device_id={"mem": peer}, device_id_type=MESH,
        )

    def share(buf, send, recv, slot, other, peer):
        return pltpu.make_async_remote_copy(
            src_ref=buf.at[slot], dst_ref=buf.at[slot], send_sem=send.at[other],
            recv_sem=recv.at[slot], device_id={"band": peer}, device_id_type=MESH,
        )

    def columns(peer):
        return pl.ds(pl.multiple_of(peer * width, width), width)

    def forth(f, peer, src):
        return pltpu.make_async_remote_copy(
            src_ref=st.at[f, :, :, columns(peer)], dst_ref=xb.at[f, src], send_sem=fs_sem.at[f, peer],
            recv_sem=fr_sem.at[f, src], device_id={"mem": peer}, device_id_type=MESH,
        )

    def forth_one(f, m, peer):
        return pltpu.make_async_remote_copy(
            src_ref=st.at[f, m, :, columns(peer)], dst_ref=xb.at[f, me, m], send_sem=fs_sem.at[f, peer],
            recv_sem=fr_sem.at[f, me], device_id={"mem": peer}, device_id_type=MESH,
        )

    def back(f, peer, src):
        return pltpu.make_async_remote_copy(
            src_ref=mb.at[f, peer], dst_ref=out.at[:, f, :, columns(src)], send_sem=bs_sem.at[f, peer],
            recv_sem=br_sem.at[f, src], device_id={"mem": peer}, device_id_type=MESH,
        )

    pl.semaphore_wait(
        barrier,
        nm - 1 + gz - 1 + gy - 1 + jnp.where(far_above, 1, 0) + jnp.where(far_below, 1, 0),
    )

    small[0].wait()
    load[V].wait()

    @pl.loop(0, members)
    def _(m):
        flux = depth[...] * st[V, m]
        dv[m] = flux
        edges(0, m, flux)

    def flat(x):
        return jnp.concatenate([x[q : q + 1, :] for q in range(x.shape[0])], axis=1)

    small[4].wait()
    slot = rows_of((PAD, n_obs))
    own_noise = jnp.zeros((PAD, n_obs), jnp.float32)
    for m in range(members):
        own_noise = jnp.where(slot == m, flat(pert[m]), own_noise)
    noise[me] = own_noise
    for peer in mates:
        tell(noise, ns_sem, nr_sem, peer, me).start()

    load[U].wait()
    load[H].wait()

    @pl.loop(0, members)
    def _(m):
        st[H, m] = st[H, m] - 0.25 * east(depth[...] * st[U, m])

    @pl.loop(0, members)
    def _(m):
        arrive(0, m)
        h = st[H, m] - 0.25 * north(dv[m], hr[0, 0, m], hr[0, 1, m])
        st[H, m] = h
        edges(1, m, h)
        st[U, m] = st[U, m] - 0.25 * east(h) + turn(cols) * st[V, m]
        for peer in mates:
            forth_one(U, m, peer).start()

    for copy in small[1:4]:
        copy.wait()

    local = flat(pos[...]) - b * (rows * cols)
    obs_row = lax.shift_right_logical(local, int(math.log2(cols)))
    obs_col = jnp.bitwise_and(local, cols - 1)
    step = 256

    @pl.loop(0, cols // step)
    def _(k):
        col = rows_of((step, n_obs)) + k * step
        onehot[pl.ds(pl.multiple_of(k * step, step), step), :] = jnp.where(
            col == obs_col, 1.0, 0.0
        ).astype(jnp.bfloat16)

    @pl.loop(0, members)
    def _(m):
        arrive(1, m)
        v = st[V, m] - 0.25 * north(st[H, m], hr[1, 0, m], hr[1, 1, m]) - turn(cols) * st[U, m]
        st[V, m] = v
        flux = depth[...] * v
        dv[m] = flux
        edges(2, m, flux)

    @pl.loop(0, members)
    def _(m):
        h = st[H, m] - 0.25 * east(depth[...] * st[U, m])
        arrive(2, m)
        st[H, m] = h - 0.25 * north(dv[m], hr[2, 0, m], hr[2, 1, m])

    tall = members * rows
    kstep = 512

    def pick(k, acc):
        at = pl.ds(pl.multiple_of(k * kstep, kstep), kstep)
        h = st[H, :, :, at].reshape(tall, kstep)
        hi = h.astype(jnp.bfloat16)
        rest = h - hi.astype(jnp.float32)
        mid = rest.astype(jnp.bfloat16)
        low = (rest - mid.astype(jnp.float32)).astype(jnp.bfloat16)
        hb[0:tall] = hi
        hb[tall : 2 * tall] = mid
        hb[2 * tall : 3 * tall] = low
        return acc + jnp.dot(hb[...], onehot[at, :], preferred_element_type=jnp.float32)

    picked = lax.fori_loop(0, cols // kstep, pick, jnp.zeros((3 * tall, n_obs), jnp.float32))
    picked = picked[0:tall] + (picked[tall : 2 * tall] + picked[2 * tall : 3 * tall])
    here = rows_of((rows, n_obs)) == obs_row
    own = jnp.zeros((PAD, n_obs), jnp.float32)
    for m in range(members):
        mine = jnp.where(here, picked[m * rows : (m + 1) * rows], 0.0)
        own = jnp.where(slot == m, jnp.sum(mine, axis=0, keepdims=True), own)
    pi[me] = own
    for peer in mates:
        tell(pi, as_sem, ar_sem, peer, me).start()
    for f in range(3):
        xb[f, me] = st[f, :, :, columns(me)]

    j = lax.shift_right_logical(rows_of((cells, np_)), int(math.log2(rows)))
    padded = j
    for k in range(1, nm):
        padded = padded + jnp.where(j >= k * members, PAD - members, 0)
    spread_rows[...] = jnp.where(lanes_of((cells, np_)) == padded, 1.0, 0.0).astype(jnp.bfloat16)

    err = flat(scale[...])
    factor = jnp.full((1, n_obs), infl[0], jnp.float32)
    known = flat(obs[...])
    weight = jnp.sqrt(factor) * err
    for peer in mates:
        tell(noise, ns_sem, nr_sem, peer, peer).wait_recv()
    aimed = known + weight * noise[...].reshape(np_, n_obs)
    for peer in mates:
        tell(pi, as_sem, ar_sem, peer, peer).wait_recv()
    predicted = pi[...].reshape(np_, n_obs)
    centre = jnp.sum(predicted, axis=0, keepdims=True) * (1.0 / total)
    inside = jnp.bitwise_and(rows_of((np_, n_obs)), PAD - 1) < members
    unit = err * norm
    spread = jnp.where(inside, (predicted - centre) / unit, 0.0)
    innovation = jnp.where(inside, (aimed - predicted) / err, 0.0)
    half = nm // 2
    core = lax.rem(me, 2)
    mine = pi[pl.ds(core * half, half)].reshape(half * PAD, n_obs)
    own_spread = jnp.where(inside[0 : half * PAD], (mine - centre) / unit, 0.0)
    zb[z] = nt(own_spread, jnp.concatenate([spread, innovation], axis=0), HIGHEST)
    others = [lax.rem(z + s, gz) for s in range(1, gz)]
    for other in others:
        share(zb, zs_sem, zr_sem, z, other, y * gz + other).start()
    for peer in mates:
        forth(V, peer, me).start()
    for peer in mates:
        forth(H, peer, me).start()
    for other in others:
        share(zb, zs_sem, zr_sem, other, other, y * gz + other).wait_recv()
    yb[y] = jnp.sum(zb[...], axis=0)
    layers = [lax.rem(y + s, gy) for s in range(1, gy)]
    for other in layers:
        share(yb, ys_sem, yr_sem, y, other, other * gz + z).start()
    for other in layers:
        share(yb, ys_sem, yr_sem, other, other, other * gz + z).wait_recv()
    sb[core] = jnp.sum(yb[...], axis=0)
    swap = pltpu.make_async_remote_copy(
        src_ref=sb.at[core], dst_ref=sb.at[core], send_sem=ss_sem, recv_sem=sr_sem,
        device_id={"mem": me + 1 - 2 * core}, device_id_type=MESH,
    )
    swap.start()
    swap.wait()

    shape = (PAD, 2 * np_)
    sub, lane = rows_of(shape), lanes_of(shape)
    blocks = [
        sb[k // half, (k % half) * PAD : (k % half + 1) * PAD]
        + jnp.where(sub + k * PAD == lane, infl[0], 0.0)
        for k in range(nm)
    ]
    for k in range(total):
        home, r = divmod(k, members)
        p = home * PAD + r
        line = blocks[home][r : r + 1]
        line = line / line[:, p : p + 1]
        new = [x - x[:, p : p + 1] * line for x in blocks]
        new[home] = jnp.where(sub == r, line, new[home])
        blocks = new
    weights = jnp.concatenate([x[:, np_:] for x in blocks], axis=0)
    square = (np_, np_)
    mean = jnp.sum(weights, axis=0, keepdims=True) * (1.0 / total)
    transform = jnp.where(rows_of(square) == lanes_of(square), 1.0, 0.0) + (weights - mean) * (1.0 / norm)

    alike = jnp.bitwise_and(rows_of((cells, cells)), rows - 1) == jnp.bitwise_and(
        lanes_of((cells, cells)), rows - 1
    )

    def widen(t):
        grown = nt(spread_rows[...], t).astype(jnp.bfloat16)
        return jnp.where(alike, nt(grown, spread_rows[...]), 0.0).astype(jnp.bfloat16)

    hi = transform.astype(jnp.bfloat16)
    mix_hi = widen(hi)
    mix_lo = widen((transform - hi.astype(jnp.float32)).astype(jnp.bfloat16))

    for f in (U, H, V):
        for peer in mates:
            forth(f, peer, peer).wait_recv()
        x = xb[f].reshape(cells, width)
        x_hi = x.astype(jnp.bfloat16)
        x_lo = (x - x_hi.astype(jnp.float32)).astype(jnp.bfloat16)
        mixed = jnp.dot(mix_hi, x_hi, preferred_element_type=jnp.float32) + (
            jnp.dot(mix_hi, x_lo, preferred_element_type=jnp.float32)
            + jnp.dot(mix_lo, x_hi, preferred_element_type=jnp.float32)
        )
        mb[f] = mixed.reshape(nm, members, rows, width)
        if f == V:
            for peer in mates:
                back(H, peer, me).wait_send()
        for peer in mates:
            back(f, peer, me).start()
        out[:, f, :, columns(me)] = mb[f, me]

    for peer in mates:
        back(H, peer, peer).wait_recv()

    @pl.loop(0, members)
    def _(m):
        edges(3, m, out[m, H])

    for peer in mates:
        back(U, peer, peer).wait_recv()

    @pl.loop(0, members)
    def _(m):
        out[m, U] = out[m, U] - 0.25 * east(out[m, H])

    @pl.loop(0, members)
    def _(m):
        arrive(3, m)
        dv[m] = 0.25 * north(out[m, H], hr[3, 0, m], hr[3, 1, m])

    def finish(src):
        at = columns(src)
        f = turn(width)
        for m in range(members):
            v = out[m, V, :, at]
            u = out[m, U, :, at] + f * v
            out[m, U, :, at] = u
            out[m, V, :, at] = v - dv[m, :, at] - f * u

    finish(me)

    @pl.loop(1, nm)
    def _(s):
        peer = lax.rem(me + s, nm)
        back(V, peer, peer).wait_recv()
        finish(peer)

    @pl.loop(0, members)
    def _(m):
        for t in range(4):

            @pl.when(b > 0)
            def _():
                halo(t, 0, m).wait_send()

            @pl.when(b < nb - 1)
            def _():
                halo(t, 1, m).wait_send()

    for peer in mates:
        tell(noise, ns_sem, nr_sem, peer, me).wait_send()
        tell(pi, as_sem, ar_sem, peer, me).wait_send()
    for other in others:
        share(zb, zs_sem, zr_sem, z, other, y * gz + other).wait_send()
    for other in layers:
        share(yb, ys_sem, yr_sem, y, other, other * gz + z).wait_send()
    for peer in mates:
        for f in range(3):
            forth(f, peer, me).wait_send()
        back(U, peer, me).wait_send()
        back(V, peer, me).wait_send()


def body(ens, depth, pos, obs, scale, pert, infl):
    nm, nb = lax.axis_size("mem"), lax.axis_size("band")
    gz = 8 if nb >= 16 else 2
    gy = nb // gz
    members, fields, rows, cols = ens.shape
    n_obs = pos.size
    np_ = nm * PAD
    cells = nm * members * rows
    f32, bf16 = jnp.float32, jnp.bfloat16
    dma = pltpu.SemaphoreType.DMA
    vmem = pl.BlockSpec(memory_space=pltpu.VMEM)
    return pl.pallas_call(
        functools.partial(kernel, nm, nb, gz),
        out_shape=jax.ShapeDtypeStruct(ens.shape, f32),
        in_specs=[pl.BlockSpec(memory_space=pltpu.HBM)] * 6 + [pl.BlockSpec(memory_space=pltpu.SMEM)],
        out_specs=vmem,
        scratch_shapes=[
            pltpu.VMEM(depth.shape, f32),
            pltpu.VMEM(pos.shape, jnp.int32),
            pltpu.VMEM(obs.shape, f32),
            pltpu.VMEM(scale.shape, f32),
            pltpu.VMEM(pert.shape, f32),
            pltpu.VMEM((fields, members, rows, cols), f32),
            pltpu.VMEM((members, rows, cols), f32),
            pltpu.VMEM((4, 2, members, 1, cols), f32),
            pltpu.VMEM((4, 2, members, 1, cols), f32),
            pltpu.VMEM((cols, n_obs), bf16),
            pltpu.VMEM((3 * members * rows, 512), bf16),
            pltpu.VMEM((nm, PAD, n_obs), f32),
            pltpu.VMEM((nm, PAD, n_obs), f32),
            pltpu.VMEM((gz, np_ // 2, 2 * np_), f32),
            pltpu.VMEM((gy, np_ // 2, 2 * np_), f32),
            pltpu.VMEM((2, np_ // 2, 2 * np_), f32),
            pltpu.VMEM((fields, nm, members, rows, cols // nm), f32),
            pltpu.VMEM((fields, nm, members, rows, cols // nm), f32),
            pltpu.VMEM((cells, np_), bf16),
            dma((fields,)),
            dma((5,)),
            dma((4, 2, members)),
            dma((4, 2, members)),
            dma((nm,)),
            dma((nm,)),
            dma((nm,)),
            dma((nm,)),
            dma((gz,)),
            dma((gz,)),
            dma((gy,)),
            dma((gy,)),
            dma,
            dma,
            dma((fields, nm)),
            dma((fields, nm)),
            dma((fields, nm)),
            dma((fields, nm)),
        ],
        compiler_params=pltpu.CompilerParams(
            collective_id=0, has_side_effects=True, vmem_limit_bytes=64 * 1024 * 1024 - 65536
        ),
        name="smoother",
    )(ens, depth, pos, obs, scale, pert, infl)


def solution(mesh):
    in_specs = (
        P("mem", None, "band", None),
        P("band", None),
        P("band", None),
        P("band", None),
        P("band", None),
        P("mem", "band", None),
        P(),
    )
    out_specs = P("mem", None, "band", None)
    return jax.shard_map(body, mesh=mesh, in_specs=in_specs, out_specs=out_specs, check_vma=False)
```

time: 87.5 us -> 82.1 us (0.938)
  local copies, waits for them, and re-layouts: 6.72 us -> 3.27 us
  Pallas kernels: 79.9 us -> 78.1 us
    unnamed x13 -> x1, local copies, waits for them, and re-layouts: 6.72 us -> 3.27 us
    pallas_call x1, Pallas kernels: 79.9 us -> 78.1 us  [body(): pl.pallas_call(functools.partial(kernel, nm, nb, gz), out_shape=jax.Shape...]
where the time goes in v2:
time: 82.1 us; the launch traced here: 82 us
  Pallas kernels  78.1 us (95%)
  local copies, waits for them, and re-layouts  3.27 us (4%)
    pallas_call x1, Pallas kernels, body(): pl.pallas_call(functools.partial(kernel, nm, nb, gz), out_shape=jax.Shape...  78.1 us
    unnamed x1, local copies, waits for them, and re-layouts  3.27 us

profile of v2, /device:TPU:1, one launch (start us, length us, event | category | flops | bytes accessed | tf_op | source)
XLA Modules:
  0.0 82.0 jit_solution(8500792514558229170)
XLA Ops:
  0.7 78.1 %smoother.1 = f32[6,3,8,4096]{3,2,1,0:T(8,128)} custom-call(f32[6,3,8,4096]{3,2,1,0:T(8,128)} %ens.1, f32[8,4096]{1,0:T(8,128)} %depth_in.1, s32[4,128]{1,0:T(4,128)} %pos_in.1, f32[4,128]{1,0:T(4,128)} %obs_in.1, f32[4,128]{1,0:T(4,128)} %scale_in.1, f32[6,4,128]{2,1,0:T(4,128)} %pert_in.1, f32[1]{0:T(128)S(6)} %copy.9.infl), custom_call_target="tpu_custom_call" | custom-call | tf_op jit(solution)/shard_map/smoother/pallas_call | solution.py:454
  78.7 3.3 %copy.10 = f32[6,3,8,4096]{3,2,1,0:T(8,128)} copy(f32[6,3,8,4096]{3,2,1,0:T(8,128)} %smoother.1) | data formatting | bytes 4718592

commit v3 on v2

--- a/solution.py
+++ b/solution.py
@@ -496,10 +496,10 @@
             dma((fields, nm)),
         ],
         compiler_params=pltpu.CompilerParams(
-            collective_id=0, has_side_effects=True, vmem_limit_bytes=64 * 1024 * 1024 - 65536
+            collective_id=0, has_side_effects=True, vmem_limit_bytes=48 * 1024 * 1024
         ),
         name="smoother",
-    )(ens, depth, pos, obs, scale, pert, infl)
+    )(*[pltpu.with_memory_space_constraint(x, pltpu.HBM) for x in (ens, depth, pos, obs, scale, pert)], infl)
 
 
 def solution(mesh):

time: 82.1 us -> 78.8 us (0.960)
  local copies, waits for them, and re-layouts: 3.27 us -> 1.41 us
  Pallas kernels: 78.1 us -> 76.7 us
    unnamed x1, local copies, waits for them, and re-layouts: 3.27 us -> 1.41 us
    pallas_call x1, Pallas kernels: 78.1 us -> 76.7 us  [body(): pl.pallas_call(functools.partial(kernel, nm, nb, gz), out_shape=jax.Shape...]
where the time goes in v3:
time: 78.8 us; the launch traced here: 78.7 us
  Pallas kernels  76.7 us (97%)
  local copies, waits for them, and re-layouts  1.41 us (2%)
    pallas_call x1, Pallas kernels, body(): pl.pallas_call(functools.partial(kernel, nm, nb, gz), out_shape=jax.Shape...  76.7 us

profile of v3, /device:TPU:1, one launch (start us, length us, event | category | flops | bytes accessed | tf_op | source)
XLA Modules:
  0.0 78.7 jit_solution(2417276102962961390)
XLA Ops:
  0.7 76.7 %smoother.1 = f32[6,3,8,4096]{3,2,1,0:T(8,128)S(1)} custom-call(f32[6,3,8,4096]{3,2,1,0:T(8,128)} %ens.1, f32[8,4096]{1,0:T(8,128)} %depth_in.1, s32[4,128]{1,0:T(4,128)} %pos_in.1, f32[4,128]{1,0:T(4,128)} %obs_in.1, f32[4,128]{1,0:T(4,128)} %scale_in.1, f32[6,4,128]{2,1,0:T(4,128)} %pert_in.1, f32[1]{0:T(128)S(6)} %copy.9.infl), custom_call_target="tpu_custom_call" | custom-call | tf_op jit(solution)/shard_map/smoother/pallas_call | solution.py:454
  77.3 1.4 %copy.10 = f32[6,3,8,4096]{3,2,1,0:T(8,128)} copy(f32[6,3,8,4096]{3,2,1,0:T(8,128)S(1)} %smoother.1) | data formatting | bytes 4718592

commit v4 on v3

--- a/solution.py
+++ b/solution.py
@@ -335,13 +335,19 @@
         + jnp.where(sub + k * PAD == lane, infl[0], 0.0)
         for k in range(nm)
     ]
-    for k in range(total):
+    for k in range(0, total, 2):
         home, r = divmod(k, members)
         p = home * PAD + r
-        line = blocks[home][r : r + 1]
-        line = line / line[:, p : p + 1]
-        new = [x - x[:, p : p + 1] * line for x in blocks]
-        new[home] = jnp.where(sub == r, line, new[home])
+        one, two = blocks[home][r : r + 1], blocks[home][r + 1 : r + 2]
+        def lanes(x, at):
+            return jnp.broadcast_to(x[:, at : at + 1], x.shape)
+
+        a, c, d, e = lanes(one, p), lanes(one, p + 1), lanes(two, p), lanes(two, p + 1)
+        scale_ = 1.0 / (a * e - c * d)
+        first = (e * scale_) * one - (c * scale_) * two
+        second = (a * scale_) * two - (d * scale_) * one
+        new = [x - x[:, p : p + 1] * first - x[:, p + 1 : p + 2] * second for x in blocks]
+        new[home] = jnp.where(sub == r, first, jnp.where(sub == r + 1, second, new[home]))
         blocks = new
     weights = jnp.concatenate([x[:, np_:] for x in blocks], axis=0)
     square = (np_, np_)

time: 78.8 us -> 77.2 us (0.980)
  Pallas kernels: 76.7 us -> 75 us
    pallas_call x1, Pallas kernels: 76.7 us -> 75 us  [body(): pl.pallas_call(functools.partial(kernel, nm, nb, gz), out_shape=jax.Shape...]
where the time goes in v4:
time: 77.2 us; the launch traced here: 77.1 us
  Pallas kernels  75 us (97%)
  local copies, waits for them, and re-layouts  1.41 us (2%)
    pallas_call x1, Pallas kernels, body(): pl.pallas_call(functools.partial(kernel, nm, nb, gz), out_shape=jax.Shape...  75 us

profile of v4, /device:TPU:1, one launch (start us, length us, event | category | flops | bytes accessed | tf_op | source)
XLA Modules:
  0.0 77.1 jit_solution(6131995333249704069)
XLA Ops:
  0.7 75.0 %smoother.1 = f32[6,3,8,4096]{3,2,1,0:T(8,128)S(1)} custom-call(f32[6,3,8,4096]{3,2,1,0:T(8,128)} %ens.1, f32[8,4096]{1,0:T(8,128)} %depth_in.1, s32[4,128]{1,0:T(4,128)} %pos_in.1, f32[4,128]{1,0:T(4,128)} %obs_in.1, f32[4,128]{1,0:T(4,128)} %scale_in.1, f32[6,4,128]{2,1,0:T(4,128)} %pert_in.1, f32[1]{0:T(128)S(6)} %copy.9.infl), custom_call_target="tpu_custom_call" | custom-call | tf_op jit(solution)/shard_map/smoother/pallas_call | solution.py:460
  75.7 1.4 %copy.10 = f32[6,3,8,4096]{3,2,1,0:T(8,128)} copy(f32[6,3,8,4096]{3,2,1,0:T(8,128)S(1)} %smoother.1) | data formatting | bytes 4718592

commit v5 on v4

--- a/solution.py
+++ b/solution.py
@@ -252,7 +252,7 @@
         st[H, m] = h - 0.25 * north(dv[m], hr[2, 0, m], hr[2, 1, m])
 
     tall = members * rows
-    kstep = 512
+    kstep = cols // 2
 
     def pick(k, acc):
         at = pl.ds(pl.multiple_of(k * kstep, kstep), kstep)
@@ -473,7 +473,7 @@
             pltpu.VMEM((4, 2, members, 1, cols), f32),
             pltpu.VMEM((4, 2, members, 1, cols), f32),
             pltpu.VMEM((cols, n_obs), bf16),
-            pltpu.VMEM((3 * members * rows, 512), bf16),
+            pltpu.VMEM((3 * members * rows, cols // 2), bf16),
             pltpu.VMEM((nm, PAD, n_obs), f32),
             pltpu.VMEM((nm, PAD, n_obs), f32),
             pltpu.VMEM((gz, np_ // 2, 2 * np_), f32),

time: 77.2 us -> 76.1 us (0.986)
  Pallas kernels: 75 us -> 73.9 us
    pallas_call x1, Pallas kernels: 75 us -> 73.9 us  [body(): pl.pallas_call(functools.partial(kernel, nm, nb, gz), out_shape=jax.Shape...]
where the time goes in v5:
time: 76.1 us; the launch traced here: 76 us
  Pallas kernels  73.9 us (97%)
  local copies, waits for them, and re-layouts  1.41 us (2%)
    pallas_call x1, Pallas kernels, body(): pl.pallas_call(functools.partial(kernel, nm, nb, gz), out_shape=jax.Shape...  73.9 us

profile of v5, /device:TPU:1, one launch (start us, length us, event | category | flops | bytes accessed | tf_op | source)
XLA Modules:
  0.0 76.0 jit_solution(2776825344038087522)
XLA Ops:
  0.7 73.9 %smoother.1 = f32[6,3,8,4096]{3,2,1,0:T(8,128)S(1)} custom-call(f32[6,3,8,4096]{3,2,1,0:T(8,128)} %ens.1, f32[8,4096]{1,0:T(8,128)} %depth_in.1, s32[4,128]{1,0:T(4,128)} %pos_in.1, f32[4,128]{1,0:T(4,128)} %obs_in.1, f32[4,128]{1,0:T(4,128)} %scale_in.1, f32[6,4,128]{2,1,0:T(4,128)} %pert_in.1, f32[1]{0:T(128)S(6)} %copy.9.infl), custom_call_target="tpu_custom_call" | custom-call | tf_op jit(solution)/shard_map/smoother/pallas_call | solution.py:460
  74.6 1.4 %copy.10 = f32[6,3,8,4096]{3,2,1,0:T(8,128)} copy(f32[6,3,8,4096]{3,2,1,0:T(8,128)S(1)} %smoother.1) | data formatting | bytes 4718592

commit v6 on v5

--- a/solution.py
+++ b/solution.py
@@ -252,7 +252,7 @@
         st[H, m] = h - 0.25 * north(dv[m], hr[2, 0, m], hr[2, 1, m])
 
     tall = members * rows
-    kstep = cols // 2
+    kstep = cols
 
     def pick(k, acc):
         at = pl.ds(pl.multiple_of(k * kstep, kstep), kstep)
@@ -473,7 +473,7 @@
             pltpu.VMEM((4, 2, members, 1, cols), f32),
             pltpu.VMEM((4, 2, members, 1, cols), f32),
             pltpu.VMEM((cols, n_obs), bf16),
-            pltpu.VMEM((3 * members * rows, cols // 2), bf16),
+            pltpu.VMEM((3 * members * rows, cols), bf16),
             pltpu.VMEM((nm, PAD, n_obs), f32),
             pltpu.VMEM((nm, PAD, n_obs), f32),
             pltpu.VMEM((gz, np_ // 2, 2 * np_), f32),

time: 76.1 us -> 75.8 us (level)
  no operation moved by 1% of the time
where the time goes in v6:
time: 75.8 us; the launch traced here: 75.7 us
  Pallas kernels  73.7 us (97%)
  local copies, waits for them, and re-layouts  1.41 us (2%)
    pallas_call x1, Pallas kernels, body(): pl.pallas_call(functools.partial(kernel, nm, nb, gz), out_shape=jax.Shape...  73.7 us

profile of v6, /device:TPU:1, one launch (start us, length us, event | category | flops | bytes accessed | tf_op | source)
XLA Modules:
  0.0 75.7 jit_solution(12275994709368119228)
XLA Ops:
  0.7 73.7 %smoother.1 = f32[6,3,8,4096]{3,2,1,0:T(8,128)S(1)} custom-call(f32[6,3,8,4096]{3,2,1,0:T(8,128)} %ens.1, f32[8,4096]{1,0:T(8,128)} %depth_in.1, s32[4,128]{1,0:T(4,128)} %pos_in.1, f32[4,128]{1,0:T(4,128)} %obs_in.1, f32[4,128]{1,0:T(4,128)} %scale_in.1, f32[6,4,128]{2,1,0:T(4,128)} %pert_in.1, f32[1]{0:T(128)S(6)} %copy.9.infl), custom_call_target="tpu_custom_call" | custom-call | tf_op jit(solution)/shard_map/smoother/pallas_call | solution.py:460
  74.3 1.4 %copy.10 = f32[6,3,8,4096]{3,2,1,0:T(8,128)} copy(f32[6,3,8,4096]{3,2,1,0:T(8,128)S(1)} %smoother.1) | data formatting | bytes 4718592
